TPU v7x, 256 devices: a whole 4x4x8 slice. The times are simulated.
256 devices in a mesh: dp: 8 (over x, z_lo), seq: 32 (over y, z_hi, core).
Axes of the slice: x: 4, y: 4, z: 8 (z_hi: 4, z_lo: 2; z = z_hi * 2 + z_lo), core: 2. Of those that a mesh axis runs over, the one named last changes fastest.
Arguments:
- queries: bfloat16 [8, 32, 512, 1024], P('dp', 'seq'), may hold values from -16 to 16
- keys: bfloat16 [8, 32, 512, 1024], P('dp', 'seq'), may hold values from -12 to 12
- values: bfloat16 [8, 32, 512, 1024], P('dp', 'seq'), may hold values from -24 to 24
- out_proj: bfloat16 [1024, 2048], P(('dp', 'seq')), may hold values from -0.1875 to 0.1875
- out_grad: bfloat16 [8, 32, 512, 2048], P('dp', 'seq'), may hold values from -48 to 48
- block_pattern: int32 [4, 4], replicated, may hold values from 0 to 3, as said below
- col_offset: int32 [4], replicated, may hold values from 0 to 511
Outputs:
- layer_out: bfloat16 [8, 32, 512, 2048], P('dp', 'seq')
- q_grad: bfloat16 [8, 32, 512, 1024], P('dp', 'seq')
- k_grad: bfloat16 [8, 32, 512, 1024], P('dp', 'seq')
- v_grad: bfloat16 [8, 32, 512, 1024], P('dp', 'seq')
- w_grad: float32 [1024, 2048], P(('dp', 'seq'))
Inputs may be any that keep to these rules, and one draw needn't show every extreme that they name: `block_pattern`: for each row head, the entries name each of the 4 blocks of a grid row once, and entry j is never j.
All inputs are finite; a program needn't handle non-finite values.
Results may differ from a plain program's by a relative error of at most 0.006.
Values may be sent and summed in bfloat16 or wider, within the bound.
No kernel may reach another device: no remote copies, remote signals or barrier semaphores. Data moves between devices by JAX's collectives and lax.ppermute only.
A program may use at most 128 MiB of HBM per device.

v0:
```python
import jax
import jax.numpy as jnp
from jax import lax
from jax.sharding import PartitionSpec as P

HD = 128
HR = 4
HC = 4
BLK = 128
NB = 4


def block_selector(block_pattern):
    numbers = jnp.arange(NB, dtype=jnp.int32)
    return (block_pattern.T[:, :, None] == numbers[None, None, :]).astype(jnp.bfloat16)


def roll_columns(tensor, col_offset, direction):
    moved_heads = [
        jnp.roll(tensor[:, :, head_idx], direction * col_offset[head_idx], axis=1)
        for head_idx in range(HC)
    ]
    return jnp.stack(moved_heads, axis=2)


def column_forward(parts):
    query_cols, key_cols, value_cols = parts
    score_scale = HD ** (-0.5)
    scores = (
        jnp.einsum("rchd,schd->rchs", query_cols, key_cols, preferred_element_type=jnp.float32)
        * score_scale
    )
    col_probs = jax.nn.softmax(scores, axis=-1)
    col_out = jnp.einsum(
        "rchs,schd->rchd",
        col_probs.astype(jnp.bfloat16),
        value_cols,
        preferred_element_type=jnp.float32,
    ).astype(jnp.bfloat16)
    return (col_out, col_probs, query_cols, key_cols, value_cols)


def column_backward(query_cols, key_cols, value_cols, col_probs, grad_cols):
    score_scale = HD ** (-0.5)
    prob_half = col_probs.astype(jnp.bfloat16)
    value_grad = jnp.einsum(
        "rchs,rchd->schd", prob_half, grad_cols, preferred_element_type=jnp.float32
    ).astype(jnp.bfloat16)
    prob_grad = jnp.einsum(
        "rchd,schd->rchs", grad_cols, value_cols, preferred_element_type=jnp.float32
    )
    delta_sum = jnp.sum(col_probs * prob_grad, axis=-1, keepdims=True)
    score_grad = (col_probs * (prob_grad - delta_sum)).astype(jnp.bfloat16)
    query_grad = (
        jnp.einsum("rchs,schd->rchd", score_grad, key_cols, preferred_element_type=jnp.float32)
        * score_scale
    ).astype(jnp.bfloat16)
    key_grad = (
        jnp.einsum("rchs,rchd->schd", score_grad, query_cols, preferred_element_type=jnp.float32)
        * score_scale
    ).astype(jnp.bfloat16)
    return (query_grad, key_grad, value_grad)


def row_forward(query_rows, key_rows, value_rows, selector):
    score_scale = HD ** (-0.5)
    key_other = jnp.einsum(
        "jhm,rmbhd->rjbhd", selector, key_rows, preferred_element_type=jnp.float32
    ).astype(jnp.bfloat16)
    value_other = jnp.einsum(
        "jhm,rmbhd->rjbhd", selector, value_rows, preferred_element_type=jnp.float32
    ).astype(jnp.bfloat16)
    key_joined = jnp.concatenate([key_other, key_rows], axis=2)
    value_joined = jnp.concatenate([value_other, value_rows], axis=2)
    scores = (
        jnp.einsum("rjqhd,rjkhd->rjhqk", query_rows, key_joined, preferred_element_type=jnp.float32)
        * score_scale
    )
    row_probs = jax.nn.softmax(scores, axis=-1)
    row_out = jnp.einsum(
        "rjhqk,rjkhd->rjqhd",
        row_probs.astype(jnp.bfloat16),
        value_joined,
        preferred_element_type=jnp.float32,
    ).astype(jnp.bfloat16)
    return (row_out, row_probs, key_joined, value_joined)


def fold_back(term_sums, selector):
    own_part = term_sums[:, :, BLK:]
    moved_part = jnp.einsum(
        "jhm,rjbhd->rmbhd",
        selector.astype(jnp.float32),
        term_sums[:, :, :BLK],
        precision=lax.Precision.HIGHEST,
    )
    return (own_part + moved_part).astype(jnp.bfloat16)


def row_backward(query_rows, key_joined, value_joined, row_probs, grad_rows, selector):
    score_scale = HD ** (-0.5)
    prob_half = row_probs.astype(jnp.bfloat16)
    value_terms = jnp.einsum(
        "rjhqk,rjqhd->rjkhd", prob_half, grad_rows, preferred_element_type=jnp.float32
    )
    prob_grad = jnp.einsum(
        "rjqhd,rjkhd->rjhqk", grad_rows, value_joined, preferred_element_type=jnp.float32
    )
    delta_sum = jnp.sum(row_probs * prob_grad, axis=-1, keepdims=True)
    score_grad = (row_probs * (prob_grad - delta_sum)).astype(jnp.bfloat16)
    query_grad = (
        jnp.einsum("rjhqk,rjkhd->rjqhd", score_grad, key_joined, preferred_element_type=jnp.float32)
        * score_scale
    ).astype(jnp.bfloat16)
    key_terms = (
        jnp.einsum("rjhqk,rjqhd->rjkhd", score_grad, query_rows, preferred_element_type=jnp.float32)
        * score_scale
    )
    return (query_grad, fold_back(key_terms, selector), fold_back(value_terms, selector))


def shards(queries, keys, values, out_proj, out_grad, block_pattern, col_offset):
    row_count = queries.shape[1]
    col_count = queries.shape[2]
    feat_width = queries.shape[3]
    model_width = out_grad.shape[3]
    head_count = feat_width // HD
    token_count = row_count * col_count
    query_heads = queries.reshape(row_count, col_count, head_count, HD)
    key_heads = keys.reshape(row_count, col_count, head_count, HD)
    value_heads = values.reshape(row_count, col_count, head_count, HD)
    selector = block_selector(block_pattern)
    grad_flat = out_grad.reshape(token_count, model_width)
    attn_grad = lax.dot_general(
        grad_flat,
        lax.all_gather(out_proj, ("dp", "seq"), axis=0, tiled=True),
        (((1,), (1,)), ((), ())),
        preferred_element_type=jnp.float32,
    ).astype(jnp.bfloat16)
    grad_heads = attn_grad.reshape(row_count, col_count, head_count, HD)
    key_shift = roll_columns(key_heads[:, :, HR:], col_offset, 1)
    value_shift = roll_columns(value_heads[:, :, HR:], col_offset, 1)
    row_shape = (row_count, NB, BLK, HR, HD)
    query_rows = query_heads[:, :, :HR].reshape(row_shape)
    col_out, col_probs, query_cols, key_cols, value_cols = column_forward(
        (
            lax.all_to_all(query_heads[:, :, HR:], "seq", split_axis=1, concat_axis=0, tiled=True),
            lax.all_to_all(key_shift, "seq", split_axis=1, concat_axis=0, tiled=True),
            lax.all_to_all(value_shift, "seq", split_axis=1, concat_axis=0, tiled=True),
        )
    )
    row_out, row_probs, key_joined, value_joined = row_forward(
        query_rows,
        key_heads[:, :, :HR].reshape(row_shape),
        value_heads[:, :, :HR].reshape(row_shape),
        selector,
    )
    col_back = lax.all_to_all(col_out, "seq", split_axis=0, concat_axis=1, tiled=True)
    grad_cols = lax.all_to_all(
        grad_heads[:, :, HR:], "seq", split_axis=1, concat_axis=0, tiled=True
    )
    col_query_grad, col_key_grad, col_value_grad = column_backward(
        query_cols, key_cols, value_cols, col_probs, grad_cols
    )
    query_back, key_back, value_back = (
        lax.all_to_all(col_query_grad, "seq", split_axis=0, concat_axis=1, tiled=True),
        lax.all_to_all(col_key_grad, "seq", split_axis=0, concat_axis=1, tiled=True),
        lax.all_to_all(col_value_grad, "seq", split_axis=0, concat_axis=1, tiled=True),
    )
    attention = jnp.concatenate(
        [row_out.reshape(row_count, col_count, HR, HD), col_back], axis=2
    ).reshape(token_count, feat_width)
    attn_part = attention
    layer_sum = jnp.dot(
        attn_part,
        lax.all_gather(out_proj, ("dp", "seq"), axis=0, tiled=True),
        preferred_element_type=jnp.float32,
    )
    data_count = lax.axis_size("dp")
    seq_count = lax.axis_size("seq")
    attn_part = attention
    summed_grad = lax.psum_scatter(
        lax.dot_general(
            attn_part, grad_flat, (((0,), (0,)), ((), ())), preferred_element_type=jnp.float32
        ),
        ("dp", "seq"),
        scatter_dimension=0,
        tiled=True,
    )
    w_grad = summed_grad * (data_count * seq_count * token_count) ** (-0.5)
    key_back = roll_columns(key_back, col_offset, -1)
    value_back = roll_columns(value_back, col_offset, -1)
    row_query_grad, row_key_grad, row_value_grad = row_backward(
        query_rows,
        key_joined,
        value_joined,
        row_probs,
        grad_heads[:, :, :HR].reshape(row_shape),
        selector,
    )

    def assemble(row_part, col_part):
        return jnp.concatenate(
            [row_part.reshape(row_count, col_count, HR, HD), col_part], axis=2
        ).reshape(1, row_count, col_count, feat_width)

    layer_out = layer_sum.astype(jnp.bfloat16).reshape(1, row_count, col_count, model_width)
    return (
        layer_out,
        assemble(row_query_grad, query_back),
        assemble(row_key_grad, key_back),
        assemble(row_value_grad, value_back),
        w_grad,
    )


def solution(mesh):
    in_specs = (
        P("dp", "seq", None, None),
        P("dp", "seq", None, None),
        P("dp", "seq", None, None),
        P(("dp", "seq"), None),
        P("dp", "seq", None, None),
        P(),
        P(),
    )
    out_specs = (
        P("dp", "seq", None, None),
        P("dp", "seq", None, None),
        P("dp", "seq", None, None),
        P("dp", "seq", None, None),
        P(("dp", "seq"), None),
    )
    return jax.shard_map(shards, mesh=mesh, in_specs=in_specs, out_specs=out_specs, check_vma=False)
```

profile of v0, /device:TPU:1, one launch (start us, length us, event | category | flops | bytes accessed | tf_op | source)
XLA Modules:
  0.0 978.9 jit_solution(12304957022160518582)
XLA Ops:
  12.0 12.8 %all-to-all-start.2 = ((bf16[1,512,4,128]{3,2,0,1:T(4,128)(2,1)}), bf16[1,512,4,128]{3,2,0,1:T(4,128)(2,1)}, u32[]{:S(2)}, u32[]{:S(2)}) async-start(bf16[1,512,4,128]{3,2,0,1:T(4,128)(2,1)} %copy.246), calls=%async_computation.2 | async-start | bytes 1048576 | tf_op jit(solution)/shard_map/all_to_all | solution.py:147
  58.5 9.8 %all-to-all-start.1 = ((bf16[1,512,4,128]{3,2,0,1:T(4,128)(2,1)}), bf16[1,512,4,128]{3,2,0,1:T(4,128)(2,1)}, u32[]{:S(2)}, u32[]{:S(2)}) async-start(bf16[1,512,4,128]{3,2,0,1:T(4,128)(2,1)} %copy.244), calls=%async_computation.1 | async-start | bytes 1048576 | tf_op jit(solution)/shard_map/all_to_all | solution.py:148
  70.5 15.7 %all-to-all-done.1 = bf16[1,512,4,128]{3,2,0,1:T(4,128)(2,1)} async-done(((bf16[1,512,4,128]{3,2,0,1:T(4,128)(2,1)}), bf16[1,512,4,128]{3,2,0,1:T(4,128)(2,1)}, u32[]{:S(2)}, u32[]{:S(2)}) %all-to-all-start.1) | async-done | bytes 524320 | tf_op jit(solution)/shard_map/all_to_all | solution.py:148
  86.2 6.3 all-to-all-start
  102.9 2.7 maximum_bitcast_fusion
  110.7 2.8 fusion.122
  117.5 10.0 %all-to-all-start.3 = ((bf16[32,16,4,128]{3,2,1,0:T(4,128)(2,1)}), bf16[32,16,4,128]{3,2,1,0:T(4,128)(2,1)}, u32[]{:S(2)}, u32[]{:S(2)}) async-start(bf16[32,16,4,128]{3,2,1,0:T(4,128)(2,1)} %copy.252), calls=%async_computation.3 | async-start | bytes 1048576 | tf_op jit(solution)/shard_map/all_to_all | solution.py:158
  132.8 12.5 %all-to-all-done.3 = bf16[32,16,4,128]{3,2,1,0:T(4,128)(2,1)} async-done(((bf16[32,16,4,128]{3,2,1,0:T(4,128)(2,1)}), bf16[32,16,4,128]{3,2,1,0:T(4,128)(2,1)}, u32[]{:S(2)}, u32[]{:S(2)}) %all-to-all-start.3) | async-done | bytes 524320 | tf_op jit(solution)/shard_map/all_to_all | solution.py:158
  150.9 6.8 fusion.3
  161.1 270.5 %all-reduce.3.cloned.1.call-done = f32[1024,2048]{1,0:T(8,128)} async-done(((f32[1024,2048]{1,0:T(8,128)}), f32[1024,2048]{1,0:T(8,128)}) %all-reduce.3.cloned.1.call-update) | async-done | bytes 8388624
  433.1 413.8 %all-gather.3.cloned.1.call-done = bf16[256,4,2048]{2,1,0:T(4,128)(2,1)} async-done(((bf16[1,4,2048]{2,1,0:T(4,128)(2,1)}), bf16[256,4,2048]{2,1,0:T(4,128)(2,1)}) %all-gather.3.cloned.1.call-update) | async-done | bytes 4194320 | tf_op jit(solution)/shard_map/all_gather | solution.py:176
  846.9 6.9 reshape.197
  853.8 4.5 fusion.16
  860.8 8.3 all-to-all-start.4
  878.3 8.8 all-to-all-done.4
  892.5 5.3 all-to-all-start.5
  902.6 3.3 fusion.113
  905.9 2.6 copy.283
  912.3 3.5 all-to-all-done.5
  915.8 6.5 all-to-all-start.6
  923.6 6.0 fusion.2
  931.0 9.3 all-to-all-done.6
  940.4 4.8 all-to-all-start.7
  954.3 8.9 all-to-all-done.7
  (161 shorter events, 111.2 us)
Async XLA Ops:
  7.2 143.7 %copy-start = (bf16[1,1,512,2048]{3,2,1,0:T(8,128)(2,1)S(1)}, bf16[1,1,512,2048]{3,2,1,0:T(8,128)(2,1)}, u32[]{:S(2)}) copy-start(bf16[1,1,512,2048]{3,2,1,0:T(8,128)(2,1)} %param.13) | copy-start | bytes 6291460
  8.8 16.0 %copy-start.28 = (s32[4]{0:T(128)S(1)}, s32[4]{0:T(128)}, u32[]{:S(2)}) copy-start(s32[4]{0:T(128)} %param.15) | copy-start | bytes 52
  12.0 46.5 %all-to-all-start.2 = ((bf16[1,512,4,128]{3,2,0,1:T(4,128)(2,1)}), bf16[1,512,4,128]{3,2,0,1:T(4,128)(2,1)}, u32[]{:S(2)}, u32[]{:S(2)}) async-start(bf16[1,512,4,128]{3,2,0,1:T(4,128)(2,1)} %copy.246), calls=%async_computation.2 | async-start | bytes 1048576 | tf_op jit(solution)/shard_map/all_to_all | solution.py:147
  53.0 15.3 %copy-start.24 = (bf16[1,512,1,128]{3,1,2,0:T(8,128)(2,1)S(1)}, bf16[1,512,1,128]{3,1,2,0:T(8,128)(2,1)}, u32[]{:S(2)}) copy-start(bf16[1,512,1,128]{3,1,2,0:T(8,128)(2,1)} %get-tuple-element.52) | copy-start | bytes 393220
  55.1 13.2 %copy-start.25 = (bf16[1,512,1,128]{3,1,2,0:T(8,128)(2,1)S(1)}, bf16[1,512,1,128]{3,1,2,0:T(8,128)(2,1)}, u32[]{:S(2)}) copy-start(bf16[1,512,1,128]{3,1,2,0:T(8,128)(2,1)} %get-tuple-element.54) | copy-start | bytes 393220
  57.2 11.1 %copy-start.26 = (bf16[1,512,1,128]{3,1,2,0:T(8,128)(2,1)S(1)}, bf16[1,512,1,128]{3,1,2,0:T(8,128)(2,1)}, u32[]{:S(2)}) copy-start(bf16[1,512,1,128]{3,1,2,0:T(8,128)(2,1)} %get-tuple-element.56) | copy-start | bytes 393220
  58.5 27.8 %all-to-all-start.1 = ((bf16[1,512,4,128]{3,2,0,1:T(4,128)(2,1)}), bf16[1,512,4,128]{3,2,0,1:T(4,128)(2,1)}, u32[]{:S(2)}, u32[]{:S(2)}) async-start(bf16[1,512,4,128]{3,2,0,1:T(4,128)(2,1)} %copy.244), calls=%async_computation.1 | async-start | bytes 1048576 | tf_op jit(solution)/shard_map/all_to_all | solution.py:148
  86.2 27.3 %all-to-all-start = ((bf16[1,512,4,128]{3,2,0,1:T(4,128)(2,1)}), bf16[1,512,4,128]{3,2,0,1:T(4,128)(2,1)}, u32[]{:S(2)}, u32[]{:S(2)}) async-start(bf16[1,512,4,128]{3,2,0,1:T(4,128)(2,1)} %copy.238), calls=%async_computation | async-start | bytes 1048576 | tf_op jit(solution)/shard_map/all_to_all | solution.py:149
  96.6 5.8 copy-start.27
  117.5 27.9 %all-to-all-start.3 = ((bf16[32,16,4,128]{3,2,1,0:T(4,128)(2,1)}), bf16[32,16,4,128]{3,2,1,0:T(4,128)(2,1)}, u32[]{:S(2)}, u32[]{:S(2)}) async-start(bf16[32,16,4,128]{3,2,1,0:T(4,128)(2,1)} %copy.252), calls=%async_computation.3 | async-start | bytes 1048576 | tf_op jit(solution)/shard_map/all_to_all | solution.py:158
  127.5 304.1 %all-reduce.3.cloned.1.call-start = ((), (), s32[]{:S(2)}) async-start(), calls=%async_computation.9 | async-start | bytes 16777216
  157.8 689.1 %all-gather.3.cloned.1.call-start = ((), (), s32[]{:S(2)}) async-start(), calls=%async_computation.8 | async-start | bytes 4210688 | tf_op jit(solution)/shard_map/all_gather | solution.py:176
  859.7 11.0 %copy-start.3 = (f32[4,4,128,256]{2,3,1,0:T(8,128)S(1)}, f32[4,4,128,256]{2,3,1,0:T(8,128)}, u32[]{:S(2)}) copy-start(f32[4,4,128,256]{2,3,1,0:T(8,128)} %copy-done.2) | copy-start | bytes 6291460
  860.8 26.3 %all-to-all-start.4 = ((bf16[1,512,4,128]{3,2,0,1:T(4,128)(2,1)}), bf16[1,512,4,128]{3,2,0,1:T(4,128)(2,1)}, u32[]{:S(2)}, u32[]{:S(2)}) async-start(bf16[1,512,4,128]{3,2,0,1:T(4,128)(2,1)} %slice.155), calls=%async_computation.4 | async-start | bytes 1048576 | tf_op jit(solution)/shard_map/all_to_all | solution.py:159
  876.5 11.8 %copy-start.18 = (f32[32,16,4,32]{0,3,2,1:T(8,128)S(1)}, f32[32,16,4,32]{0,3,2,1:T(8,128)}, u32[]{:S(2)}) copy-start(f32[32,16,4,32]{0,3,2,1:T(8,128)} %get-tuple-element.44) | copy-start | bytes 786436
  892.5 23.3 %all-to-all-start.5 = ((bf16[32,16,4,128]{3,2,1,0:T(4,128)(2,1)}), bf16[32,16,4,128]{3,2,1,0:T(4,128)(2,1)}, u32[]{:S(2)}, u32[]{:S(2)}) async-start(bf16[32,16,4,128]{3,2,1,0:T(4,128)(2,1)} %copy.269), calls=%async_computation.5 | async-start | bytes 1048576 | tf_op jit(solution)/shard_map/all_to_all | solution.py:166
  905.9 5.1 copy-start.7
  915.8 24.5 %all-to-all-start.6 = ((bf16[32,16,4,128]{3,2,1,0:T(4,128)(2,1)}), bf16[32,16,4,128]{3,2,1,0:T(4,128)(2,1)S(1)}, u32[]{:S(2)}, u32[]{:S(2)}) async-start(bf16[32,16,4,128]{3,2,1,0:T(4,128)(2,1)} %copy.277), calls=%async_computation.6 | async-start | bytes 1048576 | tf_op jit(solution)/shard_map/all_to_all | solution.py:167
  923.6 6.0 copy-start.20
  923.6 6.0 copy-start.23
  929.9 15.2 %copy-start.10 = (bf16[1,4,128,4,128]{4,2,1,3,0:T(8,128)(2,1)S(1)}, bf16[1,4,128,4,128]{4,2,1,3,0:T(8,128)(2,1)}, u32[]{:S(2)}) copy-start(bf16[1,4,128,4,128]{4,2,1,3,0:T(8,128)(2,1)} %copy.275) | copy-start | bytes 1572868
  929.9 16.1 %copy-start.9 = (bf16[1,4,128,4,128]{2,4,3,1,0:T(8,128)(2,1)S(1)}, bf16[1,4,128,4,128]{2,4,3,1,0:T(8,128)(2,1)}, u32[]{:S(2)}) copy-start(bf16[1,4,128,4,128]{2,4,3,1,0:T(8,128)(2,1)} %fusion.32) | copy-start | bytes 1572868
  940.4 6.0 copy-start.11
  940.4 22.9 %all-to-all-start.7 = ((bf16[32,16,4,128]{3,2,1,0:T(4,128)(2,1)}), bf16[32,16,4,128]{3,2,1,0:T(4,128)(2,1)}, u32[]{:S(2)}, u32[]{:S(2)}) async-start(bf16[32,16,4,128]{3,2,1,0:T(4,128)(2,1)} %copy.286), calls=%async_computation.7 | async-start | bytes 1048576 | tf_op jit(solution)/shard_map/all_to_all | solution.py:168
  (15 other events, 27.2 us)
Sparse Core Ops, SparseCore 0:
  157.9 273.6 all-reduce.2
  433.6 413.1 all-gather.2
where the time goes:
time: 986 us; the launch traced here: 979 us
  waiting for transfers between devices  744 us (75%)
  local copies, waits for them, and re-layouts  82 us (8%)
  starting transfers between devices  64 us (6%)
  matrix products  36.2 us (4%)
  other arithmetic  27.8 us (3%)
  between operations  25.1 us (3%)
    all_gather x1, waiting for transfers between devices, shards(): lax.all_gather(out_proj, ('dp', 'seq'), axis=0, tiled=True)  414 us
    unnamed x3, waiting for transfers between devices  271 us
    unnamed x69, local copies, waits for them, and re-layouts  22.3 us
  transfers between devices with their start and end apart: 10, of which 8 were waited for; matrix products, arithmetic and copies ran while one was open for 10% of the time, Pallas kernels for 0%

commit v1 on v0

--- a/solution.py
+++ b/solution.py
@@ -120,6 +120,16 @@
 
 
 def shards(queries, keys, values, out_proj, out_grad, block_pattern, col_offset):
+
+    def define_grid(packet, mesh_name):
+        h_now = lax.all_to_all(
+            jnp.stack(lax.axis_size(mesh_name) * [packet], axis=0),
+            axis_name=mesh_name,
+            split_axis=0,
+            concat_axis=0,
+        )
+        return jnp.concatenate(h_now, axis=0)
+
     row_count = queries.shape[1]
     col_count = queries.shape[2]
     feat_width = queries.shape[3]
@@ -172,9 +182,7 @@
     ).reshape(token_count, feat_width)
     attn_part = attention
     layer_sum = jnp.dot(
-        attn_part,
-        lax.all_gather(out_proj, ("dp", "seq"), axis=0, tiled=True),
-        preferred_element_type=jnp.float32,
+        attn_part, define_grid(out_proj, ("dp", "seq")), preferred_element_type=jnp.float32
     )
     data_count = lax.axis_size("dp")
     seq_count = lax.axis_size("seq")

time: 986 us -> 960 us (0.974)
  waiting for transfers between devices: 744 us -> 686 us
  local copies, waits for them, and re-layouts: 82 us -> 97.1 us
  starting transfers between devices: 64 us -> 75.5 us
    all_gather x1, waiting for transfers between devices: 414 us -> 299 us  [shards(): lax.all_gather(out_proj, ('dp', 'seq'), axis=0, tiled=True)]
    unnamed x3, waiting for transfers between devices: 271 us -> 325 us
    all_to_all x1, waiting for transfers between devices: 0.01 us -> 15.9 us  [shards(): lax.all_to_all(query_heads[:, :, HR:], 'seq', split_axis=1, concat_axis=0...]
    all_to_all x1, waiting for transfers between devices: 12.5 us -> 0.01 us  [shards(): lax.all_to_all(col_out, 'seq', split_axis=0, concat_axis=1, tiled=True)]
    unnamed x69 -> x71, local copies, waits for them, and re-layouts: 22.3 us -> 23.9 us
  transfers between devices with their start and end apart: 10 -> 11, of which waited for: 8 -> 9; matrix products, arithmetic and copies ran while one was open for 10% -> 15% of each run, Pallas kernels for 0% -> 0%
where the time goes in v1:
time: 960 us; the launch traced here: 949 us
  waiting for transfers between devices  686 us (71%)
  local copies, waits for them, and re-layouts  97.1 us (10%)
  starting transfers between devices  75.5 us (8%)
  matrix products  39.7 us (4%)
  other arithmetic  25.6 us (3%)
  between operations  25.2 us (3%)
    unnamed x3, waiting for transfers between devices  325 us
    all_gather x1, waiting for transfers between devices, shards(): lax.all_gather(out_proj, ('dp', 'seq'), axis=0, tiled=True)  299 us
    unnamed x71, local copies, waits for them, and re-layouts  23.9 us
  transfers between devices with their start and end apart: 11, of which 9 were waited for; matrix products, arithmetic and copies ran while one was open for 15% of the time, Pallas kernels for 0%

profile of v1, /device:TPU:1, one launch (start us, length us, event | category | flops | bytes accessed | tf_op | source)
XLA Modules:
  0.0 948.8 jit_solution(10483223710782579403)
XLA Ops:
  42.3 12.8 %all-to-all-start.1 = ((bf16[1,512,4,128]{3,2,0,1:T(4,128)(2,1)}), bf16[1,512,4,128]{3,2,0,1:T(4,128)(2,1)}, u32[]{:S(2)}, u32[]{:S(2)}) async-start(bf16[1,512,4,128]{3,2,0,1:T(4,128)(2,1)} %copy.244), calls=%async_computation.1 | async-start | bytes 1048576 | tf_op jit(solution)/shard_map/all_to_all | solution.py:158
  61.8 12.1 %all-to-all-done.1 = bf16[1,512,4,128]{3,2,0,1:T(4,128)(2,1)} async-done(((bf16[1,512,4,128]{3,2,0,1:T(4,128)(2,1)}), bf16[1,512,4,128]{3,2,0,1:T(4,128)(2,1)}, u32[]{:S(2)}, u32[]{:S(2)}) %all-to-all-start.1) | async-done | bytes 524320 | tf_op jit(solution)/shard_map/all_to_all | solution.py:158
  73.9 4.8 all-to-all-start.2
  80.9 15.9 %all-to-all-done.2 = bf16[1,512,4,128]{3,2,0,1:T(4,128)(2,1)} async-done(((bf16[1,512,4,128]{3,2,0,1:T(4,128)(2,1)}), bf16[1,512,4,128]{3,2,0,1:T(4,128)(2,1)}, u32[]{:S(2)}, u32[]{:S(2)}) %all-to-all-start.2) | async-done | bytes 524320 | tf_op jit(solution)/shard_map/all_to_all | solution.py:157
  96.8 5.2 all-to-all-start
  127.7 8.2 all-to-all-start.3
  138.4 299.4 %all-gather.3.cloned.1.call-done = bf16[256,4,2048]{2,1,0:T(4,128)(2,1)} async-done(((bf16[1,4,2048]{2,1,0:T(4,128)(2,1)}), bf16[256,4,2048]{2,1,0:T(4,128)(2,1)}) %all-gather.3.cloned.1.call-update) | async-done | bytes 4194320 | tf_op jit(solution)/shard_map/all_gather | solution.py:146
  437.8 6.9 reshape.203
  444.7 4.5 fusion.16
  451.7 13.5 %all-to-all-start.5 = ((bf16[1,512,4,128]{3,2,0,1:T(4,128)(2,1)}), bf16[1,512,4,128]{3,2,0,1:T(4,128)(2,1)}, u32[]{:S(2)}, u32[]{:S(2)}) async-start(bf16[1,512,4,128]{3,2,0,1:T(4,128)(2,1)} %slice.155), calls=%async_computation.5 | async-start | bytes 1048576 | tf_op jit(solution)/shard_map/all_to_all | solution.py:169
  474.7 8.5 all-to-all-done.5
  483.2 4.2 stack.48
  487.3 9.9 %all-to-all-start.4 = ((bf16[256,4,2048]{2,1,0:T(4,128)(2,1)}), bf16[256,4,2048]{2,1,0:T(4,128)(2,1)}, u32[]{:S(2)}, u32[]{:S(2)}) async-start(bf16[256,4,2048]{2,1,0:T(4,128)(2,1)} %stack.48), calls=%async_computation.4 | async-start | bytes 8388608 | tf_op jit(solution)/shard_map/all_to_all | solution.py:125
  497.4 6.8 fusion.3
  507.0 324.0 %all-reduce.3.cloned.1.call-done = f32[1024,2048]{1,0:T(8,128)} async-done(((f32[1024,2048]{1,0:T(8,128)}), f32[1024,2048]{1,0:T(8,128)}) %all-reduce.3.cloned.1.call-update) | async-done | bytes 8388624
  839.7 3.3 fusion.113
  861.0 10.7 %all-to-all-start.8 = ((bf16[32,16,4,128]{3,2,1,0:T(4,128)(2,1)}), bf16[32,16,4,128]{3,2,1,0:T(4,128)(2,1)}, u32[]{:S(2)}, u32[]{:S(2)}) async-start(bf16[32,16,4,128]{3,2,1,0:T(4,128)(2,1)} %copy.286), calls=%async_computation.8 | async-start | bytes 1048576 | tf_op jit(solution)/shard_map/all_to_all | solution.py:178
  873.5 7.0 reshape.189
  884.9 4.7 all-to-all-done.8
  889.6 5.5 all-to-all-start.7
  895.2 6.3 fusion.2
  904.5 8.4 all-to-all-done.7
  912.9 4.7 all-to-all-start.6
  926.1 9.6 %all-to-all-done.6 = bf16[32,16,4,128]{3,2,1,0:T(4,128)(2,1)} async-done(((bf16[32,16,4,128]{3,2,1,0:T(4,128)(2,1)}), bf16[32,16,4,128]{3,2,1,0:T(4,128)(2,1)}, u32[]{:S(2)}, u32[]{:S(2)}) %all-to-all-start.6) | async-done | bytes 524320 | tf_op jit(solution)/shard_map/all_to_all | solution.py:176
  (167 shorter events, 126.8 us)
Async XLA Ops:
  7.2 437.5 %copy-start = (bf16[1,1,512,2048]{3,2,1,0:T(8,128)(2,1)S(1)}, bf16[1,1,512,2048]{3,2,1,0:T(8,128)(2,1)}, u32[]{:S(2)}) copy-start(bf16[1,1,512,2048]{3,2,1,0:T(8,128)(2,1)} %param.13) | copy-start | bytes 6291460
  7.2 430.6 %all-gather.3.cloned.1.call-start = ((), (), s32[]{:S(2)}) async-start(), calls=%async_computation.9 | async-start | bytes 4210688 | tf_op jit(solution)/shard_map/all_gather | solution.py:146
  42.3 31.6 %all-to-all-start.1 = ((bf16[1,512,4,128]{3,2,0,1:T(4,128)(2,1)}), bf16[1,512,4,128]{3,2,0,1:T(4,128)(2,1)}, u32[]{:S(2)}, u32[]{:S(2)}) async-start(bf16[1,512,4,128]{3,2,0,1:T(4,128)(2,1)} %copy.244), calls=%async_computation.1 | async-start | bytes 1048576 | tf_op jit(solution)/shard_map/all_to_all | solution.py:158
  57.4 21.3 %copy-start.25 = (bf16[1,512,1,128]{3,1,2,0:T(8,128)(2,1)S(1)}, bf16[1,512,1,128]{3,1,2,0:T(8,128)(2,1)}, u32[]{:S(2)}) copy-start(bf16[1,512,1,128]{3,1,2,0:T(8,128)(2,1)} %get-tuple-element.54) | copy-start | bytes 393220
  57.4 21.3 %copy-start.26 = (bf16[1,512,1,128]{3,1,2,0:T(8,128)(2,1)S(1)}, bf16[1,512,1,128]{3,1,2,0:T(8,128)(2,1)}, u32[]{:S(2)}) copy-start(bf16[1,512,1,128]{3,1,2,0:T(8,128)(2,1)} %get-tuple-element.56) | copy-start | bytes 393220
  57.4 21.3 %copy-start.27 = (bf16[1,512,1,128]{3,1,2,0:T(8,128)(2,1)S(1)}, bf16[1,512,1,128]{3,1,2,0:T(8,128)(2,1)}, u32[]{:S(2)}) copy-start(bf16[1,512,1,128]{3,1,2,0:T(8,128)(2,1)} %get-tuple-element.58) | copy-start | bytes 393220
  73.9 22.9 %all-to-all-start.2 = ((bf16[1,512,4,128]{3,2,0,1:T(4,128)(2,1)}), bf16[1,512,4,128]{3,2,0,1:T(4,128)(2,1)}, u32[]{:S(2)}, u32[]{:S(2)}) async-start(bf16[1,512,4,128]{3,2,0,1:T(4,128)(2,1)} %copy.246), calls=%async_computation.2 | async-start | bytes 1048576 | tf_op jit(solution)/shard_map/all_to_all | solution.py:157
  96.8 23.4 %all-to-all-start = ((bf16[1,512,4,128]{3,2,0,1:T(4,128)(2,1)}), bf16[1,512,4,128]{3,2,0,1:T(4,128)(2,1)}, u32[]{:S(2)}, u32[]{:S(2)}) async-start(bf16[1,512,4,128]{3,2,0,1:T(4,128)(2,1)} %copy.238), calls=%async_computation | async-start | bytes 1048576 | tf_op jit(solution)/shard_map/all_to_all | solution.py:159
  127.7 324.0 %all-to-all-start.3 = ((bf16[32,16,4,128]{3,2,1,0:T(4,128)(2,1)}), bf16[32,16,4,128]{3,2,1,0:T(4,128)(2,1)}, u32[]{:S(2)}, u32[]{:S(2)}) async-start(bf16[32,16,4,128]{3,2,1,0:T(4,128)(2,1)} %copy.252), calls=%async_computation.3 | async-start | bytes 1048576 | tf_op jit(solution)/shard_map/all_to_all | solution.py:168
  451.7 31.5 %all-to-all-start.5 = ((bf16[1,512,4,128]{3,2,0,1:T(4,128)(2,1)}), bf16[1,512,4,128]{3,2,0,1:T(4,128)(2,1)}, u32[]{:S(2)}, u32[]{:S(2)}) async-start(bf16[1,512,4,128]{3,2,0,1:T(4,128)(2,1)} %slice.155), calls=%async_computation.5 | async-start | bytes 1048576 | tf_op jit(solution)/shard_map/all_to_all | solution.py:169
  471.3 11.8 %copy-start.28 = (bf16[4,2048]{1,0:T(4,128)(2,1)S(1)}, bf16[4,2048]{1,0:T(4,128)(2,1)}, u32[]{:S(2)}) copy-start(bf16[4,2048]{1,0:T(4,128)(2,1)} %param.12) | copy-start | bytes 49156
  487.3 373.7 %all-to-all-start.4 = ((bf16[256,4,2048]{2,1,0:T(4,128)(2,1)}), bf16[256,4,2048]{2,1,0:T(4,128)(2,1)}, u32[]{:S(2)}, u32[]{:S(2)}) async-start(bf16[256,4,2048]{2,1,0:T(4,128)(2,1)} %stack.48), calls=%async_computation.4 | async-start | bytes 8388608 | tf_op jit(solution)/shard_map/all_to_all | solution.py:125
  497.2 333.8 %all-reduce.3.cloned.1.call-start = ((), (), s32[]{:S(2)}) async-start(), calls=%async_computation.10 | async-start | bytes 16777216
  504.3 329.7 %copy-start.4 = (f32[4,4,128,256]{2,3,1,0:T(8,128)S(1)}, f32[4,4,128,256]{2,3,1,0:T(8,128)}, u32[]{:S(2)}) copy-start(f32[4,4,128,256]{2,3,1,0:T(8,128)} %copy-done.3) | copy-start | bytes 6291460
  859.9 11.8 %copy-start.15 = (bf16[1,4,128,4,128]{4,2,1,3,0:T(8,128)(2,1)S(1)}, bf16[1,4,128,4,128]{4,2,1,3,0:T(8,128)(2,1)}, u32[]{:S(2)}) copy-start(bf16[1,4,128,4,128]{4,2,1,3,0:T(8,128)(2,1)} %copy.284) | copy-start | bytes 1572868
  859.9 11.9 %copy-start.13 = (bf16[1,4,128,4,128]{4,2,3,1,0:T(8,128)(2,1)S(1)}, bf16[1,4,128,4,128]{4,2,3,1,0:T(8,128)(2,1)}, u32[]{:S(2)}) copy-start(bf16[1,4,128,4,128]{4,2,3,1,0:T(8,128)(2,1)} %fusion.33) | copy-start | bytes 1572868
  859.9 12.7 %copy-start.12 = (bf16[1,4,128,4,128]{4,2,3,1,0:T(8,128)(2,1)S(1)}, bf16[1,4,128,4,128]{4,2,3,1,0:T(8,128)(2,1)}, u32[]{:S(2)}) copy-start(bf16[1,4,128,4,128]{4,2,3,1,0:T(8,128)(2,1)} %fusion.29) | copy-start | bytes 1572868
  861.0 28.6 %all-to-all-start.8 = ((bf16[32,16,4,128]{3,2,1,0:T(4,128)(2,1)}), bf16[32,16,4,128]{3,2,1,0:T(4,128)(2,1)}, u32[]{:S(2)}, u32[]{:S(2)}) async-start(bf16[32,16,4,128]{3,2,1,0:T(4,128)(2,1)} %copy.286), calls=%async_computation.8 | async-start | bytes 1048576 | tf_op jit(solution)/shard_map/all_to_all | solution.py:178
  873.5 7.0 copy-start.16
  873.5 7.0 copy-start.22
  889.6 23.3 %all-to-all-start.7 = ((bf16[32,16,4,128]{3,2,1,0:T(4,128)(2,1)}), bf16[32,16,4,128]{3,2,1,0:T(4,128)(2,1)}, u32[]{:S(2)}, u32[]{:S(2)}) async-start(bf16[32,16,4,128]{3,2,1,0:T(4,128)(2,1)} %copy.277), calls=%async_computation.7 | async-start | bytes 1048576 | tf_op jit(solution)/shard_map/all_to_all | solution.py:177
  895.1 6.3 copy-start.10
  912.9 22.8 %all-to-all-start.6 = ((bf16[32,16,4,128]{3,2,1,0:T(4,128)(2,1)}), bf16[32,16,4,128]{3,2,1,0:T(4,128)(2,1)}, u32[]{:S(2)}, u32[]{:S(2)}) async-start(bf16[32,16,4,128]{3,2,1,0:T(4,128)(2,1)} %copy.269), calls=%async_computation.6 | async-start | bytes 1048576 | tf_op jit(solution)/shard_map/all_to_all | solution.py:176
  936.9 4.9 copy-start.1
  (17 other events, 31.0 us)
Sparse Core Ops, SparseCore 0:
  9.9 427.8 all-gather.2
  504.4 326.5 all-reduce.2
